TPU v7x, 32 devices: a whole 2x2x4 slice. The times are simulated.
32 devices in a mesh: member: 4 (over y, x), region: 8 (over z, core).
Axes of the slice: x: 2, y: 2, z: 4, core: 2. Of those that a mesh axis runs over, the one named last changes fastest.
Arguments:
- states: float32 [256, 49152], P('member', 'region'), may hold values from -6 to 6
- weights: float32 [256, 49152], P('member', 'region'), may hold values from -6 to 6
- obs_count: int32 [384], P('region'), may hold values from 0 to 32
- neighbours: int32 [384, 12], P('region'), may hold values from 0 to 383, as said below
Outputs:
- increments: float32 [256, 49152], P('member', 'region')
Inputs may be any that keep to these rules, and one draw needn't show every extreme that they name: `neighbours`: each row lists 12 distinct tiles, all within 8 tiles of its own tile counting cyclically over the 384 tiles; the list always holds the tile itself and the tiles exactly 8 before and after it, in a drawn order.
All inputs are finite; a program needn't handle non-finite values.
Results may differ from a plain program's by a relative error of at most 0.0003.
Values sent between devices are 32-bit elements; how exact they have to be, the bound alone decides.
A program may use at most 128 MiB of HBM per device.

v0:
```python
import jax
import jax.numpy as jnp
from jax import lax
from jax.experimental import pallas as pl
from jax.experimental.pallas import tpu as pltpu
from jax.sharding import PartitionSpec as P

TILE = 128
HALO_TILES = 8
TPD = 12


def extended_2(block, sides, width):
    for axis, dim in sides:
        count = lax.axis_size(axis)
        forward = [(i, i + 1) for i in range(count - 1)]
        forward.append((count - 1, 0))
        backward = [(target, source) for source, target in forward]
        low = lax.ppermute(
            lax.slice_in_dim(block, block.shape[dim] - width, None, axis=dim), axis, forward
        )
        high = lax.ppermute(lax.slice_in_dim(block, 0, width, axis=dim), axis, backward)
        block = jnp.concatenate([low, block, high], axis=dim)
    return block


def taper(offset, tile):
    rows = jnp.arange(tile, dtype=jnp.float32)
    spread = tile * offset[:, None, None] + rows[None, None, :] - rows[None, :, None]
    scaled = spread / (2.0 * tile)
    return 1.0 / (1.0 + scaled * scaled)


def shards(states, weights, obs_count, neighbours):
    member_count = lax.axis_size("member")
    region_count = lax.axis_size("region")
    member_part, local_rows = states.shape
    local_tiles = local_rows // TILE
    counts = obs_count.astype(jnp.float32)
    factor = counts / (counts + 8.0)
    scaled = (weights.reshape(member_part, local_tiles, TILE) * factor[None, :, None]).reshape(
        member_part, local_rows
    )
    stacked = jnp.stack([states, scaled])
    rim = HALO_TILES * TILE
    block = TPD * TILE
    padded = extended_2(stacked, (("region", 2),), rim)
    own_block = lax.all_to_all(stacked, "member", split_axis=2, concat_axis=1, tiled=True)
    extended = extended_2(own_block, (("member", 2),), rim)
    below, above = (
        lax.all_gather(padded[:, :, :rim], "member", axis=1, tiled=True),
        lax.all_gather(padded[:, :, rim + local_rows :], "member", axis=1, tiled=True),
    )
    position = lax.axis_index("member")
    lower = jnp.where(position == 0, below, extended[:, :, :rim])
    upper = jnp.where(position == member_count - 1, above, extended[:, :, rim + block :])
    window = jnp.concatenate([lower, extended[:, :, rim : rim + block], upper], axis=2)
    members = window.shape[1]
    anomaly = window[0] - jnp.mean(window[0], axis=0, keepdims=True)
    window_weights = window[1]
    tiles_all = TPD * member_count * region_count
    first_tile = (lax.axis_index("region") * member_count + lax.axis_index("member")) * TPD
    lists = lax.dynamic_slice_in_dim(neighbours, lax.axis_index("member") * TPD, TPD, 0)
    local_ids = (lists - first_tile + HALO_TILES) % tiles_all
    span_count = 2 * HALO_TILES + 1
    tile_places = jnp.arange(TPD, dtype=jnp.int32)
    shift_places = jnp.arange(span_count, dtype=jnp.int32)
    wanted = tile_places[:, None, None] + shift_places[None, None, :]
    keep_table = jnp.sum((local_ids[:, :, None] == wanted).astype(jnp.float32), axis=1)
    mine = anomaly[:, rim : rim + block].reshape(members, TPD, TILE)

    def add_offset(shift, total):
        others = lax.dynamic_slice_in_dim(anomaly, shift * TILE, block, 1).reshape(
            members, TPD, TILE
        )
        other_weights = lax.dynamic_slice_in_dim(window_weights, shift * TILE, block, 1).reshape(
            members, TPD, TILE
        )
        covar = jnp.einsum("mti,mtj->tij", mine, others, precision=lax.Precision.HIGHEST) / (
            members - 1.0
        )
        offset = jnp.full((TPD,), shift - HALO_TILES).astype(jnp.float32)
        keep = lax.dynamic_index_in_dim(keep_table, shift, 1, keepdims=False)
        coefficient = taper(offset, TILE) * covar * keep[:, None, None]
        return total + jnp.einsum(
            "mtj,tij->mti", other_weights, coefficient, precision=lax.Precision.HIGHEST
        )

    total = lax.fori_loop(0, span_count, add_offset, jnp.zeros((members, TPD, TILE), jnp.float32))
    returned = lax.all_to_all(
        total.reshape(members, block), "member", split_axis=0, concat_axis=1, tiled=True
    )
    return returned


BLOCK = 2 * TILE
SPAN = HALO_TILES + 1
RIM = HALO_TILES * TILE


def split(value):
    high = value.astype(jnp.bfloat16)
    return high, (value - high.astype(jnp.float32)).astype(jnp.bfloat16)


def dot(left, right):
    return jnp.dot(left, right, preferred_element_type=jnp.float32)


def fill_taper(taper_ref, members):
    rows = lax.broadcasted_iota(jnp.int32, (BLOCK, BLOCK), 0)
    columns = lax.broadcasted_iota(jnp.int32, (BLOCK, BLOCK), 1)
    for k in range(SPAN):
        spread = (columns - rows + (2 * k - HALO_TILES) * TILE).astype(jnp.float32) / (2.0 * TILE)
        taper_ref[k] = 1.0 / ((1.0 + spread * spread) * (members - 1.0))


def prepare_states(value, block, own, low_ref, high_ref, low_t_ref, high_t_ref):
    anomaly = value - jnp.mean(value, axis=0, keepdims=True)
    high_ref[block], low_ref[block] = split(anomaly)
    if own is not None:
        high_t_ref[own], low_t_ref[own] = split(anomaly.T)


def prepare_weights(value, block, weight_ref):
    high = value.astype(jnp.bfloat16).astype(jnp.float32)
    weight_ref[block] = jnp.concatenate([high, value - high], axis=0).T.astype(jnp.bfloat16)


def pair_rows(pair, ks, keep_ref, low_ref, high_ref, low_t_ref, high_t_ref, taper_ref, x_high_ref, x_low_ref):
    for spot, k in enumerate(ks):
        left_high, left_low = high_t_ref[pair], low_t_ref[pair]
        right_high, right_low = high_ref[pair + k], low_ref[pair + k]
        covar = dot(left_high, right_high) + dot(left_low, right_high) + dot(left_high, right_low)
        scaled = covar * taper_ref[k]
        for s in range(2):
            for t in range(2):
                rows, columns = slice(s * TILE, (s + 1) * TILE), slice(t * TILE, (t + 1) * TILE)
                value = scaled[rows, columns] * keep_ref[2 * pair + s, 2 * k + t + 1 - s]
                place = slice((2 * spot + t) * TILE, (2 * spot + t + 1) * TILE)
                x_high_ref[rows, place], x_low_ref[rows, place] = split(value)


def pair_apply(pair, ks, weight_ref, x_high_ref, x_low_ref):
    depth = len(ks) * BLOCK
    weight = weight_ref[pl.ds(pair + ks[0], len(ks))].reshape(depth, weight_ref.shape[2])
    total = dot(x_high_ref[:, :depth], weight) + dot(x_low_ref[:, :depth], weight)
    half = total.shape[1] // 2
    return (total[:, :half] + total[:, half:]).T


def scratch_of(members, part, pairs):
    rim = RIM // BLOCK
    blocks = pairs + 2 * rim
    bf16 = jnp.bfloat16
    return [
        pltpu.VMEM((blocks, members, BLOCK), bf16),
        pltpu.VMEM((blocks, members, BLOCK), bf16),
        pltpu.VMEM((pairs, BLOCK, members), bf16),
        pltpu.VMEM((pairs, BLOCK, members), bf16),
        pltpu.VMEM((blocks, BLOCK, 2 * part), bf16),
        pltpu.VMEM((SPAN, BLOCK, BLOCK), jnp.float32),
    ] + [pltpu.VMEM((BLOCK, SPAN * BLOCK), bf16)] * 4


def keep_table_of(neighbours, factor_window, tiles_all):
    local_tiles = neighbours.shape[0]
    first = lax.axis_index("region") * local_tiles
    own = first + jnp.arange(local_tiles, dtype=jnp.int32)
    shift = (neighbours - own[:, None] + HALO_TILES + 1) % tiles_all
    places = jnp.arange(2 * SPAN + 2, dtype=jnp.int32)
    return jnp.sum((shift[:, :, None] == places).astype(jnp.float32), axis=1)


def region_kernel(
    own_ref, weights_ref, factor_ref, keep_ref, out_ref,
    low_ref, high_ref, low_t_ref, high_t_ref, weight_ref, taper_ref, xh0, xl0, xh1, xl1,
    held, weight_rim, factor_rim,
    direct_send, direct_recv, relay_send, relay_recv, rim_send, rim_recv,
):
    part, rows = own_ref.shape
    count = rows // RIM
    per_chunk = RIM // BLOCK
    half = part // 2
    member, region = lax.axis_index("member"), lax.axis_index("region")
    regions = lax.axis_size("region")
    beside = member + 1 - 2 * lax.rem(member, 2)
    across = lax.rem(member + 2, 4)
    partners = ((beside, region), (across, region))
    above = (member, lax.rem(region + 1, regions))
    below = (member, lax.rem(region + regions - 1, regions))

    barrier = pltpu.get_barrier_semaphore()
    for device in partners + (above, below):
        pl.semaphore_signal(barrier, inc=1, device_id=device, device_id_type=pl.DeviceIdType.MESH)
    pl.semaphore_wait(barrier, 4)

    def chunk_at(step):
        return step + 1

    def copy(source, target, send, recv, device):
        return pltpu.make_async_remote_copy(
            src_ref=source, dst_ref=target, send_sem=send, recv_sem=recv,
            device_id=device, device_id_type=pl.DeviceIdType.MESH,
        )

    def columns_of(chunk):
        return pl.ds(pl.multiple_of((chunk - 1) * RIM, RIM), RIM)

    def direct(step, side):
        chunk = chunk_at(step)
        return copy(
            own_ref.at[:, columns_of(chunk)], held.at[chunk, 1 + side],
            direct_send.at[side, step], direct_recv.at[side, step], partners[side],
        )

    def relay(step, side):
        chunk = chunk_at(step)
        strip = pl.ds(side * half, half)
        return copy(
            held.at[chunk, 2 - side, strip], held.at[chunk, 3, strip],
            relay_send.at[side, step], relay_recv.at[side, step], partners[side],
        )

    def rim(up, item):
        device = above if up else below
        edge, place = (count, 0) if up else (1, count + 1)
        spot = 0 if up else 1
        columns = slice((edge - 1) * RIM, edge * RIM)
        if item == 4:
            source, target = weights_ref.at[:, columns], weight_rim.at[spot]
        elif item == 5:
            source, target = factor_ref.at[:, columns], factor_rim.at[spot]
        elif item == 0:
            source, target = own_ref.at[:, columns], held.at[place, 0]
        else:
            source, target = held.at[edge, item], held.at[place, item]
        return copy(source, target, rim_send.at[spot, item], rim_recv.at[spot, item], device)

    for step in range(2):
        for side in range(2):
            direct(step, side).start()
    for item in (0, 4, 5):
        for up in (True, False):
            rim(up, item).start()

    fill_taper(taper_ref, part * 4)

    @pl.loop(0, count * per_chunk)
    def _(block):
        columns = pl.ds(pl.multiple_of(block * BLOCK, BLOCK), BLOCK)
        prepare_weights(weights_ref[:, columns] * factor_ref[0:1, columns], block + per_chunk, weight_ref)

    def prepare_own(chunk):
        @pl.loop(0, per_chunk)
        def _(b):
            block = (chunk - 1) * per_chunk + b
            inner = pl.ds(pl.multiple_of(b * BLOCK, BLOCK), BLOCK)
            mine = own_ref[:, pl.ds(pl.multiple_of(block * BLOCK, BLOCK), BLOCK)]
            value = jnp.concatenate([mine] + [held[chunk, slot, :, inner] for slot in range(1, 4)], axis=0)
            prepare_states(value, block + per_chunk, block, low_ref, high_ref, low_t_ref, high_t_ref)

    def prepare_rim(up):
        place, spot = (0, 0) if up else (count + 1, 1)

        @pl.loop(0, per_chunk)
        def _(b):
            inner = pl.ds(pl.multiple_of(b * BLOCK, BLOCK), BLOCK)
            value = jnp.concatenate([held[place, slot, :, inner] for slot in range(4)], axis=0)
            block = place * per_chunk + b
            prepare_states(value, block, None, low_ref, high_ref, low_t_ref, high_t_ref)
            prepare_weights(weight_rim[spot, :, inner] * factor_rim[spot, 0:1, inner], block, weight_ref)

    def work(group, first, last, fresh):
        buffers = ((xh0, xl0), (xh1, xl1))
        for start in range(0, per_chunk, 2):
            todo = []
            for p in (start, start + 1):
                ks = [k for k in range(SPAN) if first <= (k + p) // per_chunk <= last]
                todo.append((group * per_chunk + p, ks, buffers[p % 2]))
            for pair, ks, held_x in todo:
                pair_rows(pair, ks, keep_ref, low_ref, high_ref, low_t_ref, high_t_ref, taper_ref, *held_x)
            for pair, ks, held_x in todo:
                columns = pl.ds(pl.multiple_of(pair * BLOCK, BLOCK), BLOCK)
                term = pair_apply(pair, ks, weight_ref, *held_x)
                out_ref[:, columns] = term if fresh else out_ref[:, columns] + term

    @pl.loop(0, count + 2)
    def _(step):
        @pl.when(step < count)
        def _():
            for side in range(2):
                direct(step, side).wait_recv()
            for side in range(2):
                relay(step, side).start()

        @pl.when(step + 2 < count)
        def _():
            for side in range(2):
                direct(step + 2, side).start()

        for first, up in ((0, False), (count - 1, True)):
            @pl.when(step == first)
            def _():
                for item in (1, 2):
                    rim(up, item).start()

        @pl.when((step >= 1) & (step <= count))
        def _():
            for side in range(2):
                relay(step - 1, side).wait_recv()

        for first, up in ((1, False), (count, True)):
            @pl.when(step == first)
            def _():
                rim(up, 3).start()

        @pl.when((step >= 1) & (step <= count))
        def _():
            prepare_own(chunk_at(step - 1))

        @pl.when(step == 1)
        def _():
            work(0, 1, 1, True)

        @pl.when((step >= 2) & (step <= count))
        def _():
            work(step - 1, 0, 1, True)

        @pl.when(step == count + 1)
        def _():
            for item in range(6):
                rim(False, item).wait_recv()
            prepare_rim(False)

        @pl.when(step >= 2)
        def _():
            work(step - 2, 2, 2, False)

    for item in range(6):
        rim(True, item).wait_recv()
    prepare_rim(True)
    work(0, 0, 0, False)

    @pl.loop(0, count)
    def _(step):
        for side in range(2):
            direct(step, side).wait_send()
            relay(step, side).wait_send()

    for up in (True, False):
        for item in range(6):
            rim(up, item).wait_send()


def region_shards(states, weights, obs_count, neighbours):
    region_count = lax.axis_size("region")
    part, local_rows = states.shape
    members = part * lax.axis_size("member")
    count = local_rows // RIM
    pairs = local_rows // BLOCK
    counts = obs_count.astype(jnp.float32)
    factor = counts / (counts + 8.0)
    factor_rows = jnp.broadcast_to(factor[None, :, None], (8, local_rows // TILE, TILE)).reshape(8, local_rows)
    keep = keep_table_of(neighbours, None, region_count * (local_rows // TILE))
    vmem = pl.BlockSpec(memory_space=pltpu.VMEM)
    dma = pltpu.SemaphoreType.DMA
    return pl.pallas_call(
        region_kernel,
        out_shape=jax.ShapeDtypeStruct((part, local_rows), jnp.float32),
        in_specs=[vmem, vmem, vmem, pl.BlockSpec(memory_space=pltpu.SMEM)],
        out_specs=vmem,
        scratch_shapes=scratch_of(members, part, pairs)
        + [
            pltpu.VMEM((count + 2, 4, part, RIM), jnp.float32),
            pltpu.VMEM((2, part, RIM), jnp.float32),
            pltpu.VMEM((2, 8, RIM), jnp.float32),
            dma((2, count)), dma((2, count)), dma((2, count)), dma((2, count)),
            dma((2, 6)), dma((2, 6)),
        ],
        compiler_params=pltpu.CompilerParams(
            collective_id=0, has_side_effects=True, vmem_limit_bytes=42 * 1024 * 1024
        ),
    )(states, weights, factor_rows, keep)


def fits(states, weights, obs_count, neighbours):
    part, local_rows = states.shape
    members = part * lax.axis_size("member")
    window = local_rows + 2 * RIM
    return (
        lax.axis_size("member") == 4
        and lax.axis_size("region") > 2
        and local_rows % RIM == 0
        and local_rows >= 3 * RIM
        and members % 128 == 0
        and part % 64 == 0
        and window * (members * 12 + part * 16) <= 46 * 1024 * 1024
    )


def either(*arguments):
    return region_shards(*arguments) if fits(*arguments) else shards(*arguments)


def solution(mesh):
    placed = (P("member", "region"), P("member", "region"), P("region"), P("region", None))
    return jax.shard_map(
        either, mesh=mesh, in_specs=placed, out_specs=P("member", "region"), check_vma=False
    )
```

profile of v0, /device:TPU:0, one launch (start us, length us, event | category | flops | bytes accessed | tf_op | source)
XLA Modules:
  0.0 82.8 jit_solution(8576149922906714847)
XLA Ops:
  0.0 0.7 add_divide_fusion
  0.7 0.7 add_select_fusion
  1.4 0.1 copy.6.keep_ref
  1.5 0.1 broadcast_bitcast_fusion
  1.6 0.0 copy-start
  1.6 1.4 %copy-done = f32[64,6144]{1,0:T(8,128)S(1)} copy-done((f32[64,6144]{1,0:T(8,128)S(1)}, f32[64,6144]{1,0:T(8,128)}, u32[]{:S(2)}) %copy-start) | copy-done | bytes 1572888
  3.0 0.0 copy-start.1
  3.0 1.4 %copy-done.1 = f32[64,6144]{1,0:T(8,128)S(1)} copy-done((f32[64,6144]{1,0:T(8,128)S(1)}, f32[64,6144]{1,0:T(8,128)}, u32[]{:S(2)}) %copy-start.1) | copy-done | bytes 1572888
  4.4 77.3 %shard_map.46 = f32[64,6144]{1,0:T(8,128)S(1)} custom-call(f32[64,6144]{1,0:T(8,128)S(1)} %copy-done, f32[64,6144]{1,0:T(8,128)S(1)} %copy-done.1, f32[8,6144]{1,0:T(8,128)S(1)} %broadcast_in_dim.15.factor_ref, f32[48,20]{1,0:T(8,128)S(1)} %copy.6.keep_ref), custom_call_target="tpu_custom_call" | custom-call | tf_op jit(solution)/shard_map/pallas_call | solution.py:368
  81.7 1.1 %copy.8 = f32[64,6144]{1,0:T(8,128)} copy(f32[64,6144]{1,0:T(8,128)S(1)} %shard_map.46) | data formatting | bytes 3145728
  (3 shorter events, 0.0 us)
Async XLA Ops:
  1.6 1.4 %copy-start = (f32[64,6144]{1,0:T(8,128)S(1)}, f32[64,6144]{1,0:T(8,128)}, u32[]{:S(2)}) copy-start(f32[64,6144]{1,0:T(8,128)} %own_ref.1) | copy-start | bytes 4718596
  3.0 1.4 %copy-start.1 = (f32[64,6144]{1,0:T(8,128)S(1)}, f32[64,6144]{1,0:T(8,128)}, u32[]{:S(2)}) copy-start(f32[64,6144]{1,0:T(8,128)} %weights_ref.1) | copy-start | bytes 4718596
where the time goes:
time: 83.1 us; the launch traced here: 82.8 us
  Pallas kernels  77.3 us (93%)
  local copies, waits for them, and re-layouts  4.13 us (5%)
  other arithmetic  1.41 us (2%)
    pallas_call x1, Pallas kernels, region_shards(): pl.pallas_call(region_kernel, out_shape=jax.ShapeDtypeStruct((part, local...  77.3 us
    unnamed x5, local copies, waits for them, and re-layouts  3.96 us

commit v1 on v0

v1 whole, which is shorter than its diff:
```python
import jax
import jax.numpy as jnp
from jax import lax
from jax.experimental import pallas as pl
from jax.experimental.pallas import tpu as pltpu
from jax.sharding import PartitionSpec as P

TILE = 128
HALO_TILES = 8
TPD = 12


def extended_2(block, sides, width):
    for axis, dim in sides:
        count = lax.axis_size(axis)
        forward = [(i, i + 1) for i in range(count - 1)]
        forward.append((count - 1, 0))
        backward = [(target, source) for source, target in forward]
        low = lax.ppermute(
            lax.slice_in_dim(block, block.shape[dim] - width, None, axis=dim), axis, forward
        )
        high = lax.ppermute(lax.slice_in_dim(block, 0, width, axis=dim), axis, backward)
        block = jnp.concatenate([low, block, high], axis=dim)
    return block


def taper(offset, tile):
    rows = jnp.arange(tile, dtype=jnp.float32)
    spread = tile * offset[:, None, None] + rows[None, None, :] - rows[None, :, None]
    scaled = spread / (2.0 * tile)
    return 1.0 / (1.0 + scaled * scaled)


def shards(states, weights, obs_count, neighbours):
    member_count = lax.axis_size("member")
    region_count = lax.axis_size("region")
    member_part, local_rows = states.shape
    local_tiles = local_rows // TILE
    counts = obs_count.astype(jnp.float32)
    factor = counts / (counts + 8.0)
    scaled = (weights.reshape(member_part, local_tiles, TILE) * factor[None, :, None]).reshape(
        member_part, local_rows
    )
    stacked = jnp.stack([states, scaled])
    rim = HALO_TILES * TILE
    block = TPD * TILE
    padded = extended_2(stacked, (("region", 2),), rim)
    own_block = lax.all_to_all(stacked, "member", split_axis=2, concat_axis=1, tiled=True)
    extended = extended_2(own_block, (("member", 2),), rim)
    below, above = (
        lax.all_gather(padded[:, :, :rim], "member", axis=1, tiled=True),
        lax.all_gather(padded[:, :, rim + local_rows :], "member", axis=1, tiled=True),
    )
    position = lax.axis_index("member")
    lower = jnp.where(position == 0, below, extended[:, :, :rim])
    upper = jnp.where(position == member_count - 1, above, extended[:, :, rim + block :])
    window = jnp.concatenate([lower, extended[:, :, rim : rim + block], upper], axis=2)
    members = window.shape[1]
    anomaly = window[0] - jnp.mean(window[0], axis=0, keepdims=True)
    window_weights = window[1]
    tiles_all = TPD * member_count * region_count
    first_tile = (lax.axis_index("region") * member_count + lax.axis_index("member")) * TPD
    lists = lax.dynamic_slice_in_dim(neighbours, lax.axis_index("member") * TPD, TPD, 0)
    local_ids = (lists - first_tile + HALO_TILES) % tiles_all
    span_count = 2 * HALO_TILES + 1
    tile_places = jnp.arange(TPD, dtype=jnp.int32)
    shift_places = jnp.arange(span_count, dtype=jnp.int32)
    wanted = tile_places[:, None, None] + shift_places[None, None, :]
    keep_table = jnp.sum((local_ids[:, :, None] == wanted).astype(jnp.float32), axis=1)
    mine = anomaly[:, rim : rim + block].reshape(members, TPD, TILE)

    def add_offset(shift, total):
        others = lax.dynamic_slice_in_dim(anomaly, shift * TILE, block, 1).reshape(
            members, TPD, TILE
        )
        other_weights = lax.dynamic_slice_in_dim(window_weights, shift * TILE, block, 1).reshape(
            members, TPD, TILE
        )
        covar = jnp.einsum("mti,mtj->tij", mine, others, precision=lax.Precision.HIGHEST) / (
            members - 1.0
        )
        offset = jnp.full((TPD,), shift - HALO_TILES).astype(jnp.float32)
        keep = lax.dynamic_index_in_dim(keep_table, shift, 1, keepdims=False)
        coefficient = taper(offset, TILE) * covar * keep[:, None, None]
        return total + jnp.einsum(
            "mtj,tij->mti", other_weights, coefficient, precision=lax.Precision.HIGHEST
        )

    total = lax.fori_loop(0, span_count, add_offset, jnp.zeros((members, TPD, TILE), jnp.float32))
    returned = lax.all_to_all(
        total.reshape(members, block), "member", split_axis=0, concat_axis=1, tiled=True
    )
    return returned


BLOCK = 2 * TILE
SPAN = HALO_TILES + 1
RIM = HALO_TILES * TILE
CHUNK = RIM // 2
REACH = HALO_TILES // 2


def split(value):
    high = value.astype(jnp.bfloat16)
    return high, (value - high.astype(jnp.float32)).astype(jnp.bfloat16)


def dot(left, right):
    return jnp.dot(left, right, preferred_element_type=jnp.float32)


def fill_taper(taper_ref, members):
    rows = lax.broadcasted_iota(jnp.int32, (BLOCK, BLOCK), 0)
    columns = lax.broadcasted_iota(jnp.int32, (BLOCK, BLOCK), 1)
    for k in range(SPAN):
        spread = (rows - columns + (2 * k - HALO_TILES) * TILE).astype(jnp.float32) / (2.0 * TILE)
        taper_ref[k] = 1.0 / ((1.0 + spread * spread) * (members - 1.0))


def keep_table_of(neighbours, tiles_all):
    local_tiles = neighbours.shape[0]
    first = lax.axis_index("region") * local_tiles
    own = first + jnp.arange(local_tiles, dtype=jnp.int32)
    shift = (neighbours - own[:, None] + HALO_TILES + 1) % tiles_all
    places = jnp.arange(2 * SPAN + 2, dtype=jnp.int32)
    return jnp.sum((shift[:, :, None] == places).astype(jnp.float32), axis=1)


def region_kernel(
    own_ref, weights_ref, factor_ref, keep_ref, out_ref,
    low_ref, high_ref, low_t_ref, high_t_ref, pair_ref, taper_ref, xh_a, xl_a, xh_b, xl_b,
    held, weight_held, weight_rim, factor_rim,
    own_sem, weight_sem, direct_send, direct_recv, relay_send, relay_recv, rim_send, rim_recv,
):
    part, rows = own_ref.shape
    count = rows // CHUNK
    half = part // 2
    pairs = rows // BLOCK
    member, region = lax.axis_index("member"), lax.axis_index("region")
    regions = lax.axis_size("region")
    beside = member + 1 - 2 * lax.rem(member, 2)
    across = lax.rem(member + 2, 4)
    partners = ((beside, region), (across, region))
    above = (member, lax.rem(region + 1, regions))
    below = (member, lax.rem(region + regions - 1, regions))
    order = (0, count - 1, 1, count - 2)
    early = len(order)

    barrier = pltpu.get_barrier_semaphore()
    for device in partners + (above, below):
        pl.semaphore_signal(barrier, inc=1, device_id=device, device_id_type=pl.DeviceIdType.MESH)
    pl.semaphore_wait(barrier, 4)

    def chunk_at(step):
        return order[step] if isinstance(step, int) and step < early else step - 2

    def copy(source, target, send, recv, device):
        return pltpu.make_async_remote_copy(
            src_ref=source, dst_ref=target, send_sem=send, recv_sem=recv,
            device_id=device, device_id_type=pl.DeviceIdType.MESH,
        )

    def columns_of(chunk):
        return pl.ds(pl.multiple_of(chunk * CHUNK, CHUNK), CHUNK)

    def strip(slot):
        return pl.ds(slot * part, part)

    def own_copy(chunk):
        return pltpu.make_async_copy(
            own_ref.at[:, columns_of(chunk)], held.at[chunk + 2, strip(0)], own_sem.at[chunk]
        )

    def direct(step, side):
        chunk = chunk_at(step)
        return copy(
            own_ref.at[:, columns_of(chunk)], held.at[chunk + 2, strip(1 + side)],
            direct_send.at[side, step], direct_recv.at[side, step], partners[side],
        )

    def relay(step, side):
        chunk = chunk_at(step)
        source, target = pl.ds((2 - side) * part + side * half, half), pl.ds(3 * part + side * half, half)
        return copy(
            held.at[chunk + 2, source], held.at[chunk + 2, target],
            relay_send.at[side, step], relay_recv.at[side, step], partners[side],
        )

    def rim(up, item):
        device = above if up else below
        spot = 0 if up else 1
        if item >= 8:
            edge = slice(rows - RIM, rows) if up else slice(0, RIM)
            source, target = ((weights_ref, weight_rim), (factor_ref, factor_rim))[item - 8]
            source, target = source.at[:, edge], target.at[spot]
        else:
            slot, edge = item // 2, item % 2
            chunk, place = (count - 2 + edge, edge) if up else (edge, count + 2 + edge)
            source = held.at[chunk + 2, strip(slot)] if slot else own_ref.at[:, columns_of(chunk)]
            target = held.at[place, strip(slot)]
        return copy(source, target, rim_send.at[spot, item], rim_recv.at[spot, item], device)

    def rim_of(step, slot):
        chunk = order[step]
        up = chunk >= count - 2
        return rim(up, 2 * slot + (chunk - count + 2 if up else chunk))

    for step in range(3):
        for side in range(2):
            direct(step, side).start()
    for item in (0, 1, 8, 9):
        for up in (True, False):
            rim(up, item).start()
    for chunk in range(count):
        own_copy(chunk).start()
    weight_copy = pltpu.make_async_copy(weights_ref, weight_held, weight_sem)
    weight_copy.start()

    fill_taper(taper_ref, part * 4)

    def prepare_weights(value, columns):
        high, low = split(value)
        pair_ref[0:part, columns] = high
        pair_ref[part : 2 * part, columns] = low

    weight_copy.wait()

    @pl.loop(0, pairs)
    def _(block):
        columns = pl.ds(pl.multiple_of(block * BLOCK, BLOCK), BLOCK)
        target = pl.ds(pl.multiple_of(block * BLOCK + RIM, BLOCK), BLOCK)
        prepare_weights(weight_held[:, columns] * factor_ref[0:1, columns], target)

    def prepare(place, own):
        for b in range(CHUNK // BLOCK):
            value = held[place, :, b * BLOCK : (b + 1) * BLOCK]
            anomaly = value - jnp.mean(value, axis=0, keepdims=True)
            block = place * (CHUNK // BLOCK) + b
            high_t_ref[block], low_t_ref[block] = split(anomaly.T)
            if own:
                high_ref[block - REACH], low_ref[block - REACH] = split(anomaly)

    def work(items, held_x, fresh):
        xh_ref, xl_ref = held_x
        for buffer, (pair, ks) in enumerate(items):
            right_high, right_low = high_ref[pair], low_ref[pair]
            for spot, k in enumerate(ks):
                left_high, left_low = high_t_ref[pair + k], low_t_ref[pair + k]
                covar = dot(left_high, right_high) + dot(left_low, right_high) + dot(left_high, right_low)
                scaled = covar * taper_ref[k]
                for t in range(2):
                    for s in range(2):
                        inner, outer = slice(t * TILE, (t + 1) * TILE), slice(s * TILE, (s + 1) * TILE)
                        value = scaled[inner, outer] * keep_ref[2 * pair + s, 2 * k + t + 1 - s]
                        place = slice(spot * BLOCK + t * TILE, spot * BLOCK + (t + 1) * TILE)
                        xh_ref[buffer, place, outer], xl_ref[buffer, place, outer] = split(value)
        for buffer, (pair, ks) in enumerate(items):
            depth = len(ks) * BLOCK
            columns = pl.ds(pl.multiple_of((pair + ks[0]) * BLOCK, BLOCK), depth)
            both = dot(pair_ref[:, columns], xh_ref[buffer, :depth])
            rest = dot(pair_ref[0:part, columns], xl_ref[buffer, :depth])
            term = both[:part] + both[part:] + rest
            target = pl.ds(pl.multiple_of(pair * BLOCK, BLOCK), BLOCK)
            out_ref[:, target] = term if fresh else out_ref[:, target] + term

    wide, narrow = (xh_a, xl_a), (xh_b, xl_b)

    def ks_of(first, last):
        return tuple(range(first, last + 1))

    def work_edge(base):
        work([(base + i, ks_of(4 - i, 7 - i)) for i in range(4)], narrow, True)

    def work_inner(chunk):
        base = 2 * chunk
        work([(base, ks_of(0, 5)), (base + 1, ks_of(0, 4))], wide, True)
        work([(base - 4 + i, ks_of(8 - i, min(9 - i, 8))) for i in range(4)], narrow, False)

    def work_rim(up):
        place = count + 2 if up else 0
        spot = 1 if up else 0
        for item in range(10):
            rim(not up, item).wait_recv()

        @pl.loop(0, 2)
        def _(edge):
            prepare(place + edge, False)

        for b in range(RIM // BLOCK):
            inner = slice(b * BLOCK, (b + 1) * BLOCK)
            target = slice((rows if up else -RIM) + RIM + b * BLOCK, (rows if up else -RIM) + RIM + (b + 1) * BLOCK)
            prepare_weights(weight_rim[spot, :, inner] * factor_rim[spot, 0:1, inner], target)
        if up:
            work([(pairs - 4 + i, ks_of(8 - i, 8)) for i in range(4)], narrow, False)
        else:
            work([(i, ks_of(0, 3 - i)) for i in range(4)], narrow, False)

    def forward(step):
        for side in range(2):
            direct(step, side).wait_recv()
        for side in range(2):
            relay(step, side).start()
        if isinstance(step, int) and step < early:
            for slot in (1, 2):
                rim_of(step, slot).start()

    for chunk in range(count):
        own_copy(chunk).wait()
    forward(0)

    for step in range(early):
        forward(step + 1)
        for side in range(2):
            direct(step + 3, side).start()
        for side in range(2):
            relay(step, side).wait_recv()
        rim_of(step, 3).start()
        prepare(order[step] + 2, True)
        if step >= 2:
            work_edge(0 if step == 2 else pairs - 4)

    @pl.loop(early, count)
    def _(step):
        @pl.when(step + 1 < count)
        def _():
            forward(step + 1)

        @pl.when(step + 3 < count)
        def _():
            for side in range(2):
                direct(step + 3, side).start()

        for side in range(2):
            relay(step, side).wait_recv()
        chunk = chunk_at(step)
        prepare(chunk + 2, True)
        work_inner(chunk)

        @pl.when(chunk == 5)
        def _():
            work_rim(False)

        @pl.when(chunk == 6)
        def _():
            work_rim(True)

        @pl.when(chunk == count - 4)
        def _():
            base = pairs - 8
            work([(base, (8,)), (base + 1, (7, 8)), (base + 4, (0, 1)), (base + 5, (0,))], narrow, False)

    base = pairs - 6
    work([(base, (6, 7, 8)), (base + 1, (5, 6, 7, 8)), (base + 2, (2, 3)), (base + 3, (1, 2))], narrow, False)
    work([(base + 4, (0, 1)), (base + 5, (0,))], wide, False)

    def sent(step):
        for side in range(2):
            direct(step, side).wait_send()
            relay(step, side).wait_send()

    for step in range(early):
        sent(step)

    @pl.loop(early, count)
    def _(step):
        sent(step)

    for up in (True, False):
        for item in range(10):
            rim(up, item).wait_send()


def region_shards(states, weights, obs_count, neighbours):
    region_count = lax.axis_size("region")
    part, local_rows = states.shape
    members = part * lax.axis_size("member")
    count = local_rows // CHUNK
    pairs = local_rows // BLOCK
    blocks = pairs + 2 * REACH
    counts = obs_count.astype(jnp.float32)
    factor = counts / (counts + 8.0)
    factor_rows = jnp.broadcast_to(factor[None, :, None], (8, local_rows // TILE, TILE)).reshape(8, local_rows)
    keep = keep_table_of(neighbours, region_count * (local_rows // TILE))
    vmem = pl.BlockSpec(memory_space=pltpu.VMEM)
    anywhere = pl.BlockSpec(memory_space=pltpu.HBM)
    dma = pltpu.SemaphoreType.DMA
    bf16, f32 = jnp.bfloat16, jnp.float32
    return pl.pallas_call(
        region_kernel,
        out_shape=jax.ShapeDtypeStruct((part, local_rows), f32),
        in_specs=[anywhere, anywhere, vmem, pl.BlockSpec(memory_space=pltpu.SMEM)],
        out_specs=vmem,
        scratch_shapes=[
            pltpu.VMEM((pairs, members, BLOCK), bf16),
            pltpu.VMEM((pairs, members, BLOCK), bf16),
            pltpu.VMEM((blocks, BLOCK, members), bf16),
            pltpu.VMEM((blocks, BLOCK, members), bf16),
            pltpu.VMEM((2 * part, blocks * BLOCK), bf16),
            pltpu.VMEM((SPAN, BLOCK, BLOCK), f32),
            pltpu.VMEM((2, 6 * BLOCK, BLOCK), bf16),
            pltpu.VMEM((2, 6 * BLOCK, BLOCK), bf16),
            pltpu.VMEM((4, 4 * BLOCK, BLOCK), bf16),
            pltpu.VMEM((4, 4 * BLOCK, BLOCK), bf16),
            pltpu.VMEM((count + 4, members, CHUNK), f32),
            pltpu.VMEM((part, local_rows), f32),
            pltpu.VMEM((2, part, RIM), f32),
            pltpu.VMEM((2, 8, RIM), f32),
            dma((count,)), dma,
            dma((2, count)), dma((2, count)), dma((2, count)), dma((2, count)),
            dma((2, 10)), dma((2, 10)),
        ],
        compiler_params=pltpu.CompilerParams(
            collective_id=0, has_side_effects=True, vmem_limit_bytes=52 * 1024 * 1024
        ),
    )(states, weights, factor_rows, keep)


def fits(states, weights, obs_count, neighbours):
    part, local_rows = states.shape
    members = part * lax.axis_size("member")
    window = local_rows + 2 * RIM
    return (
        lax.axis_size("member") == 4
        and lax.axis_size("region") > 2
        and local_rows % RIM == 0
        and local_rows >= 5 * RIM
        and members == 256
        and window * (members * 12 + part * 16) <= 46 * 1024 * 1024
    )


def either(*arguments):
    return region_shards(*arguments) if fits(*arguments) else shards(*arguments)


def solution(mesh):
    placed = (P("member", "region"), P("member", "region"), P("region"), P("region", None))
    return jax.shard_map(
        either, mesh=mesh, in_specs=placed, out_specs=P("member", "region"), check_vma=False
    )
```

time: 83.1 us -> 73.4 us (0.88)
  Pallas kernels: 77.3 us -> 70.4 us
  local copies, waits for them, and re-layouts: 4.13 us -> 1.32 us
    pallas_call x1, Pallas kernels: 77.3 us -> 70.4 us  [region_shards(): pl.pallas_call(region_kernel, out_shape=jax.ShapeDtypeStruct((part, local...]
    unnamed x5 -> x1, local copies, waits for them, and re-layouts: 3.96 us -> 1.15 us
where the time goes in v1:
time: 73.4 us; the launch traced here: 73.2 us
  Pallas kernels  70.4 us (96%)
  other arithmetic  1.41 us (2%)
  local copies, waits for them, and re-layouts  1.32 us (2%)
    pallas_call x1, Pallas kernels, region_shards(): pl.pallas_call(region_kernel, out_shape=jax.ShapeDtypeStruct((part, local...  70.4 us

profile of v1, /device:TPU:0, one launch (start us, length us, event | category | flops | bytes accessed | tf_op | source)
XLA Modules:
  0.0 73.2 jit_solution(16183200716257518802)
XLA Ops:
  0.0 0.7 add_divide_fusion
  0.7 0.7 add_select_fusion
  1.4 0.1 copy.6.keep_ref
  1.5 0.1 broadcast_bitcast_fusion
  1.6 70.4 %shard_map.46 = f32[64,6144]{1,0:T(8,128)S(1)} custom-call(f32[64,6144]{1,0:T(8,128)} %own_ref.1, f32[64,6144]{1,0:T(8,128)} %weights_ref.1, f32[8,6144]{1,0:T(8,128)S(1)} %broadcast_in_dim.15.factor_ref, f32[48,20]{1,0:T(8,128)S(1)} %copy.6.keep_ref), custom_call_target="tpu_custom_call" | custom-call | tf_op jit(solution)/shard_map/pallas_call | solution.py:388
  72.0 1.1 %copy.8 = f32[64,6144]{1,0:T(8,128)} copy(f32[64,6144]{1,0:T(8,128)S(1)} %shard_map.46) | data formatting | bytes 3145728
  (3 shorter events, 0.0 us)

commit v2 on v1

--- a/solution.py
+++ b/solution.py
@@ -117,25 +117,18 @@
         taper_ref[k] = 1.0 / ((1.0 + spread * spread) * (members - 1.0))
 
 
-def keep_table_of(neighbours, tiles_all):
-    local_tiles = neighbours.shape[0]
-    first = lax.axis_index("region") * local_tiles
-    own = first + jnp.arange(local_tiles, dtype=jnp.int32)
-    shift = (neighbours - own[:, None] + HALO_TILES + 1) % tiles_all
-    places = jnp.arange(2 * SPAN + 2, dtype=jnp.int32)
-    return jnp.sum((shift[:, :, None] == places).astype(jnp.float32), axis=1)
-
-
 def region_kernel(
-    own_ref, weights_ref, factor_ref, keep_ref, out_ref,
+    own_ref, weights_ref, count_ref, lists_ref, out_ref,
     low_ref, high_ref, low_t_ref, high_t_ref, pair_ref, taper_ref, xh_a, xl_a, xh_b, xl_b,
-    held, weight_held, weight_rim, factor_rim,
-    own_sem, weight_sem, direct_send, direct_recv, relay_send, relay_recv, rim_send, rim_recv,
+    held, weight_held, weight_rim, counts_held, lists_held, turn_ref, factor_ref, keep_ref,
+    own_sem, weight_sem, direct_send, direct_recv, relay_send, relay_recv, rim_send, rim_recv, up_sem, down_sem,
 ):
     part, rows = own_ref.shape
     count = rows // CHUNK
     half = part // 2
     pairs = rows // BLOCK
+    tiles = rows // TILE
+    rim_tiles = RIM // TILE
     member, region = lax.axis_index("member"), lax.axis_index("region")
     regions = lax.axis_size("region")
     beside = member + 1 - 2 * lax.rem(member, 2)
@@ -146,10 +139,30 @@
     order = (0, count - 1, 1, count - 2)
     early = len(order)
 
+    first, last = region == 0, region == regions - 1
+
+    def signal(semaphore, device):
+        pl.semaphore_signal(semaphore, inc=1, device_id=device, device_id_type=pl.DeviceIdType.MESH)
+
     barrier = pltpu.get_barrier_semaphore()
-    for device in partners + (above, below):
-        pl.semaphore_signal(barrier, inc=1, device_id=device, device_id_type=pl.DeviceIdType.MESH)
-    pl.semaphore_wait(barrier, 4)
+    for device in partners:
+        signal(barrier, device)
+
+    @pl.when(jnp.logical_not(last))
+    def _():
+        signal(barrier, above)
+
+    @pl.when(jnp.logical_not(first))
+    def _():
+        signal(barrier, below)
+
+    @pl.when(first | last)
+    def _():
+        pl.semaphore_wait(barrier, 3)
+
+    @pl.when(jnp.logical_not(first | last))
+    def _():
+        pl.semaphore_wait(barrier, 4)
 
     def chunk_at(step):
         return order[step] if isinstance(step, int) and step < early else step - 2
@@ -163,6 +176,13 @@
     def columns_of(chunk):
         return pl.ds(pl.multiple_of(chunk * CHUNK, CHUNK), CHUNK)
 
+    def piece(step):
+        if isinstance(step, int) and step >= count - 1:
+            inner = pl.ds((step - count + 1) * BLOCK, BLOCK)
+            return count - 3, inner, pl.ds((count - 3) * CHUNK + (step - count + 1) * BLOCK, BLOCK)
+        chunk = chunk_at(step)
+        return chunk, slice(None), columns_of(chunk)
+
     def strip(slot):
         return pl.ds(slot * part, part)
 
@@ -172,17 +192,17 @@
         )
 
     def direct(step, side):
-        chunk = chunk_at(step)
+        chunk, inner, columns = piece(step)
         return copy(
-            own_ref.at[:, columns_of(chunk)], held.at[chunk + 2, strip(1 + side)],
+            own_ref.at[:, columns], held.at[chunk + 2, strip(1 + side), inner],
             direct_send.at[side, step], direct_recv.at[side, step], partners[side],
         )
 
     def relay(step, side):
-        chunk = chunk_at(step)
+        chunk, inner, _ = piece(step)
         source, target = pl.ds((2 - side) * part + side * half, half), pl.ds(3 * part + side * half, half)
         return copy(
-            held.at[chunk + 2, source], held.at[chunk + 2, target],
+            held.at[chunk + 2, source, inner], held.at[chunk + 2, target, inner],
             relay_send.at[side, step], relay_recv.at[side, step], partners[side],
         )
 
@@ -191,8 +211,10 @@
         spot = 0 if up else 1
         if item >= 8:
             edge = slice(rows - RIM, rows) if up else slice(0, RIM)
-            source, target = ((weights_ref, weight_rim), (factor_ref, factor_rim))[item - 8]
-            source, target = source.at[:, edge], target.at[spot]
+            if item == 8:
+                source, target = weights_ref.at[:, edge], weight_rim.at[spot]
+            else:
+                source, target = count_ref, counts_held.at[1 + spot]
         else:
             slot, edge = item // 2, item % 2
             chunk, place = (count - 2 + edge, edge) if up else (edge, count + 2 + edge)
@@ -208,31 +230,77 @@
     for step in range(3):
         for side in range(2):
             direct(step, side).start()
-    for item in (0, 1, 8, 9):
+    count_copy = pltpu.make_async_copy(count_ref, counts_held.at[0], weight_sem.at[1])
+    lists_copy = pltpu.make_async_copy(lists_ref, lists_held, weight_sem.at[2])
+    weight_copy = pltpu.make_async_copy(weights_ref, weight_held, weight_sem.at[0])
+    count_copy.start()
+    lists_copy.start()
+    weight_copy.start()
+    for chunk in range(count):
+        own_copy(chunk).start()
+
+    fill_taper(taper_ref, part * 4)
+    turn_ref[...] = jnp.zeros_like(turn_ref)
+
+    @pl.when(first)
+    def _():
+        signal(up_sem, above)
+        pl.semaphore_wait(down_sem, 1)
+
+    @pl.when(last)
+    def _():
+        signal(down_sem, below)
+        pl.semaphore_wait(up_sem, 1)
+
+    @pl.when(jnp.logical_not(first | last))
+    def _():
+        pl.semaphore_wait(up_sem, 1)
+        signal(up_sem, above)
+        pl.semaphore_wait(down_sem, 1)
+        signal(down_sem, below)
+
+    for item in (0, 1, 9, 8):
         for up in (True, False):
             rim(up, item).start()
-    for chunk in range(count):
-        own_copy(chunk).start()
-    weight_copy = pltpu.make_async_copy(weights_ref, weight_held, weight_sem)
-    weight_copy.start()
-
-    fill_taper(taper_ref, part * 4)
 
     def prepare_weights(value, columns):
         high, low = split(value)
         pair_ref[0:part, columns] = high
         pair_ref[part : 2 * part, columns] = low
 
+    def factors_of(which):
+        turn_ref[0:1, 0:tiles] = counts_held[which].astype(jnp.float32)
+        spread = jnp.broadcast_to(turn_ref[...].T[0:tiles, 0:1], (tiles, TILE))
+        return spread / (spread + 8.0)
+
+    count_copy.wait()
+    factor_ref[...] = factors_of(0)
+    lists_copy.wait()
+    tiles_all = regions * tiles
+    own_tile = region * tiles + lax.broadcasted_iota(jnp.int32, lists_held.shape, 1)
+    shift = lists_held[...] - own_tile + HALO_TILES
+    shift = jnp.where(shift < 0, shift + tiles_all, jnp.where(shift >= tiles_all, shift - tiles_all, shift))
+    turn_ref[0 : shift.shape[0], 0:tiles] = shift.astype(jnp.float32)
+    turned = turn_ref[...].T
+    spreads = [jnp.broadcast_to(turned[0:tiles, i : i + 1], (tiles, TILE)) for i in range(shift.shape[0])]
+    for place in range(2 * HALO_TILES + 3):
+        total = jnp.zeros((tiles, TILE), jnp.float32)
+        for spread in spreads:
+            total = total + jnp.where(spread == place - 1.0, 1.0, 0.0)
+        keep_ref[place] = total
+
     weight_copy.wait()
 
     @pl.loop(0, pairs)
     def _(block):
-        columns = pl.ds(pl.multiple_of(block * BLOCK, BLOCK), BLOCK)
-        target = pl.ds(pl.multiple_of(block * BLOCK + RIM, BLOCK), BLOCK)
-        prepare_weights(weight_held[:, columns] * factor_ref[0:1, columns], target)
-
-    def prepare(place, own):
-        for b in range(CHUNK // BLOCK):
+        for t in range(2):
+            start = block * BLOCK + t * TILE
+            columns = pl.ds(pl.multiple_of(start, TILE), TILE)
+            target = pl.ds(pl.multiple_of(start + RIM, TILE), TILE)
+            prepare_weights(weight_held[:, columns] * factor_ref[pl.ds(2 * block + t, 1)], target)
+
+    def prepare(place, own, parts=(0, 1)):
+        for b in parts:
             value = held[place, :, b * BLOCK : (b + 1) * BLOCK]
             anomaly = value - jnp.mean(value, axis=0, keepdims=True)
             block = place * (CHUNK // BLOCK) + b
@@ -240,41 +308,80 @@
             if own:
                 high_ref[block - REACH], low_ref[block - REACH] = split(anomaly)
 
-    def work(items, held_x, fresh):
+    def put(scaled, pair, k, held_x, buffer, spot):
         xh_ref, xl_ref = held_x
-        for buffer, (pair, ks) in enumerate(items):
-            right_high, right_low = high_ref[pair], low_ref[pair]
-            for spot, k in enumerate(ks):
-                left_high, left_low = high_t_ref[pair + k], low_t_ref[pair + k]
-                covar = dot(left_high, right_high) + dot(left_low, right_high) + dot(left_high, right_low)
-                scaled = covar * taper_ref[k]
-                for t in range(2):
-                    for s in range(2):
-                        inner, outer = slice(t * TILE, (t + 1) * TILE), slice(s * TILE, (s + 1) * TILE)
-                        value = scaled[inner, outer] * keep_ref[2 * pair + s, 2 * k + t + 1 - s]
-                        place = slice(spot * BLOCK + t * TILE, spot * BLOCK + (t + 1) * TILE)
-                        xh_ref[buffer, place, outer], xl_ref[buffer, place, outer] = split(value)
-        for buffer, (pair, ks) in enumerate(items):
-            depth = len(ks) * BLOCK
-            columns = pl.ds(pl.multiple_of((pair + ks[0]) * BLOCK, BLOCK), depth)
-            both = dot(pair_ref[:, columns], xh_ref[buffer, :depth])
-            rest = dot(pair_ref[0:part, columns], xl_ref[buffer, :depth])
-            term = both[:part] + both[part:] + rest
-            target = pl.ds(pl.multiple_of(pair * BLOCK, BLOCK), BLOCK)
-            out_ref[:, target] = term if fresh else out_ref[:, target] + term
+        for t in range(2):
+            for s in range(2):
+                inner, outer = slice(t * TILE, (t + 1) * TILE), slice(s * TILE, (s + 1) * TILE)
+                value = scaled[inner, outer] * keep_ref[2 * k + t + 1 - s, pl.ds(2 * pair + s, 1)]
+                place = slice(spot * BLOCK + t * TILE, spot * BLOCK + (t + 1) * TILE)
+                xh_ref[buffer, place, outer], xl_ref[buffer, place, outer] = split(value)
+
+    def cross(pair, k, place, mirror=None):
+        left_high, left_low = high_t_ref[pair + k], low_t_ref[pair + k]
+        right_high, right_low = high_ref[pair], low_ref[pair]
+        covar = dot(left_high, right_high) + dot(left_low, right_high) + dot(left_high, right_low)
+        scaled = covar * taper_ref[k]
+        put(scaled, pair, k, *place)
+        if mirror is not None:
+            put(scaled.T, pair + k - REACH, 2 * REACH - k, *mirror)
+
+    def apply(pair, k, length, held_x, buffer, fresh, spot=0):
+        xh_ref, xl_ref = held_x
+        columns = pl.ds(pl.multiple_of((pair + k) * BLOCK, BLOCK), length * BLOCK)
+        place = slice(spot * BLOCK, (spot + length) * BLOCK)
+        both = dot(pair_ref[:, columns], xh_ref[buffer, place])
+        term = both[:part] + both[part:] + dot(pair_ref[0:part, columns], xl_ref[buffer, place])
+        target = pl.ds(pl.multiple_of(pair * BLOCK, BLOCK), BLOCK)
+        out_ref[:, target] = term if fresh else out_ref[:, target] + term
 
     wide, narrow = (xh_a, xl_a), (xh_b, xl_b)
 
-    def ks_of(first, last):
-        return tuple(range(first, last + 1))
-
     def work_edge(base):
-        work([(base + i, ks_of(4 - i, 7 - i)) for i in range(4)], narrow, True)
+        for i in range(4):
+            for j in range(i):
+                cross(base + i, REACH + j - i, (narrow, i, j), (narrow, j, i))
+            cross(base + i, REACH, (narrow, i, i))
+        for i in range(4):
+            apply(base + i, REACH - i, 4, narrow, i, True)
 
     def work_inner(chunk):
         base = 2 * chunk
-        work([(base, ks_of(0, 5)), (base + 1, ks_of(0, 4))], wide, True)
-        work([(base - 4 + i, ks_of(8 - i, min(9 - i, 8))) for i in range(4)], narrow, False)
+        for i in range(4):
+            cross(base, i, (wide, 0, i), (narrow, i, 0))
+        cross(base, 4, (wide, 0, 4))
+        cross(base, 5, (wide, 0, 5), (wide, 1, 3))
+        for i in range(3):
+            cross(base + 1, i, (wide, 1, i), (narrow, i + 1, 1))
+        cross(base + 1, 4, (wide, 1, 4))
+        apply(base, 0, 6, wide, 0, True)
+        apply(base + 1, 0, 5, wide, 1, True)
+        for i in range(4):
+            apply(base - 4 + i, 8 - i, min(i + 1, 2), narrow, i, False)
+
+    def work_close():
+        base = pairs - 8
+        cross(base, 8, (narrow, 0, 0), (narrow, 2, 0))
+        cross(base + 1, 7, (narrow, 1, 0), (narrow, 2, 1))
+        cross(base + 1, 8, (narrow, 1, 1), (narrow, 3, 0))
+        apply(base, 8, 1, narrow, 0, False)
+        apply(base + 1, 7, 2, narrow, 1, False)
+        apply(base + 4, 0, 2, narrow, 2, False)
+        apply(base + 5, 0, 1, narrow, 3, False)
+
+    def work_last(base, gap):
+        above_ks = range(REACH + 1 + gap, 2 * REACH + 1)
+        for i in range(REACH):
+            cross(base, i, (wide, 0, i), (narrow, i, 0))
+        cross(base, REACH, (wide, 0, REACH))
+        for i, k in enumerate(above_ks):
+            cross(base, k, (wide, 1, i), (narrow, i, 1))
+        apply(base, 0, REACH + 1, wide, 0, True)
+        apply(base, above_ks[0], len(above_ks), wide, 1, False)
+        for i in range(REACH):
+            apply(base - REACH + i, 2 * REACH - i, 1, narrow, i, False)
+        for i, k in enumerate(above_ks):
+            apply(base + k - REACH, 2 * REACH - k, 1, narrow, i, False, 1)
 
     def work_rim(up):
         place = count + 2 if up else 0
@@ -286,14 +393,19 @@
         def _(edge):
             prepare(place + edge, False)
 
-        for b in range(RIM // BLOCK):
-            inner = slice(b * BLOCK, (b + 1) * BLOCK)
-            target = slice((rows if up else -RIM) + RIM + b * BLOCK, (rows if up else -RIM) + RIM + (b + 1) * BLOCK)
-            prepare_weights(weight_rim[spot, :, inner] * factor_rim[spot, 0:1, inner], target)
-        if up:
-            work([(pairs - 4 + i, ks_of(8 - i, 8)) for i in range(4)], narrow, False)
-        else:
-            work([(i, ks_of(0, 3 - i)) for i in range(4)], narrow, False)
+        factors = factors_of(1 + spot)
+        for t in range(rim_tiles):
+            inner = slice(t * TILE, (t + 1) * TILE)
+            start = (rows + RIM if up else 0) + t * TILE
+            tile = t if up else tiles - rim_tiles + t
+            prepare_weights(weight_rim[spot, :, inner] * factors[tile : tile + 1], slice(start, start + TILE))
+        for i in range(4):
+            pair, first_k, length = (pairs - 4 + i, 8 - i, i + 1) if up else (i, 0, 4 - i)
+            for spot in range(length):
+                cross(pair, first_k + spot, (narrow, i, spot))
+        for i in range(4):
+            pair, first_k, length = (pairs - 4 + i, 8 - i, i + 1) if up else (i, 0, 4 - i)
+            apply(pair, first_k, length, narrow, i, False)
 
     def forward(step):
         for side in range(2):
@@ -319,16 +431,28 @@
         if step >= 2:
             work_edge(0 if step == 2 else pairs - 4)
 
-    @pl.loop(early, count)
+    ends = (count - 1, count)
+
+    @pl.loop(early, count - 1)
     def _(step):
-        @pl.when(step + 1 < count)
+        @pl.when(step + 1 < count - 1)
         def _():
             forward(step + 1)
 
-        @pl.when(step + 3 < count)
+        @pl.when(step + 3 < count - 1)
         def _():
             for side in range(2):
                 direct(step + 3, side).start()
+
+        for end in ends:
+            @pl.when(step + 3 == end)
+            def _():
+                for side in range(2):
+                    direct(end, side).start()
+
+            @pl.when(step + 1 == end)
+            def _():
+                forward(end)
 
         for side in range(2):
             relay(step, side).wait_recv()
@@ -336,32 +460,38 @@
         prepare(chunk + 2, True)
         work_inner(chunk)
 
+        @pl.when(chunk == 4)
+        def _():
+            work_rim(False)
+
         @pl.when(chunk == 5)
         def _():
-            work_rim(False)
-
-        @pl.when(chunk == 6)
-        def _():
             work_rim(True)
 
         @pl.when(chunk == count - 4)
         def _():
-            base = pairs - 8
-            work([(base, (8,)), (base + 1, (7, 8)), (base + 4, (0, 1)), (base + 5, (0,))], narrow, False)
-
-    base = pairs - 6
-    work([(base, (6, 7, 8)), (base + 1, (5, 6, 7, 8)), (base + 2, (2, 3)), (base + 3, (1, 2))], narrow, False)
-    work([(base + 4, (0, 1)), (base + 5, (0,))], wide, False)
+            work_close()
+
+    forward(ends[1])
+    for side in range(2):
+        relay(ends[0], side).wait_recv()
+    prepare(count - 1, True, (0,))
+    work_last(pairs - 6, 1)
+
+    for side in range(2):
+        relay(ends[1], side).wait_recv()
+    prepare(count - 1, True, (1,))
+    work_last(pairs - 5, 0)
 
     def sent(step):
         for side in range(2):
             direct(step, side).wait_send()
             relay(step, side).wait_send()
 
-    for step in range(early):
+    for step in tuple(range(early)) + ends:
         sent(step)
 
-    @pl.loop(early, count)
+    @pl.loop(early, count - 1)
     def _(step):
         sent(step)
 
@@ -371,16 +501,12 @@
 
 
 def region_shards(states, weights, obs_count, neighbours):
-    region_count = lax.axis_size("region")
     part, local_rows = states.shape
     members = part * lax.axis_size("member")
     count = local_rows // CHUNK
     pairs = local_rows // BLOCK
     blocks = pairs + 2 * REACH
-    counts = obs_count.astype(jnp.float32)
-    factor = counts / (counts + 8.0)
-    factor_rows = jnp.broadcast_to(factor[None, :, None], (8, local_rows // TILE, TILE)).reshape(8, local_rows)
-    keep = keep_table_of(neighbours, region_count * (local_rows // TILE))
+    tiles, listed = neighbours.shape
     vmem = pl.BlockSpec(memory_space=pltpu.VMEM)
     anywhere = pl.BlockSpec(memory_space=pltpu.HBM)
     dma = pltpu.SemaphoreType.DMA
@@ -388,7 +514,7 @@
     return pl.pallas_call(
         region_kernel,
         out_shape=jax.ShapeDtypeStruct((part, local_rows), f32),
-        in_specs=[anywhere, anywhere, vmem, pl.BlockSpec(memory_space=pltpu.SMEM)],
+        in_specs=[anywhere, anywhere, anywhere, anywhere],
         out_specs=vmem,
         scratch_shapes=[
             pltpu.VMEM((pairs, members, BLOCK), bf16),
@@ -404,15 +530,20 @@
             pltpu.VMEM((count + 4, members, CHUNK), f32),
             pltpu.VMEM((part, local_rows), f32),
             pltpu.VMEM((2, part, RIM), f32),
-            pltpu.VMEM((2, 8, RIM), f32),
-            dma((count,)), dma,
-            dma((2, count)), dma((2, count)), dma((2, count)), dma((2, count)),
+            pltpu.VMEM((3, 1, tiles), jnp.int32),
+            pltpu.VMEM((listed, tiles), jnp.int32),
+            pltpu.VMEM((TILE, TILE), f32),
+            pltpu.VMEM((tiles, TILE), f32),
+            pltpu.VMEM((2 * HALO_TILES + 3, tiles, TILE), f32),
+            dma((count,)), dma((3,)),
+            dma((2, count + 1)), dma((2, count + 1)), dma((2, count + 1)), dma((2, count + 1)),
             dma((2, 10)), dma((2, 10)),
+            pltpu.SemaphoreType.REGULAR, pltpu.SemaphoreType.REGULAR,
         ],
         compiler_params=pltpu.CompilerParams(
             collective_id=0, has_side_effects=True, vmem_limit_bytes=52 * 1024 * 1024
         ),
-    )(states, weights, factor_rows, keep)
+    )(states, weights, obs_count.reshape(1, tiles), neighbours.T)
 
 
 def fits(states, weights, obs_count, neighbours):
@@ -423,7 +554,7 @@
         lax.axis_size("member") == 4
         and lax.axis_size("region") > 2
         and local_rows % RIM == 0
-        and local_rows >= 5 * RIM
+        and 5 * RIM <= local_rows <= TILE * TILE
         and members == 256
         and window * (members * 12 + part * 16) <= 46 * 1024 * 1024
     )

time: 73.4 us -> 66.7 us (0.909)
  Pallas kernels: 70.4 us -> 64 us
  other arithmetic: 1.41 us -> 0 us
  local copies, waits for them, and re-layouts: 1.32 us -> 2.5 us
    pallas_call x1, Pallas kernels: 70.4 us -> 64 us  [region_shards(): pl.pallas_call(region_kernel, out_shape=jax.ShapeDtypeStruct((part, local...]
    unnamed x1 -> x5, local copies, waits for them, and re-layouts: 1.15 us -> 2.5 us
where the time goes in v2:
time: 66.7 us; the launch traced here: 66.5 us
  Pallas kernels  64 us (96%)
  local copies, waits for them, and re-layouts  2.5 us (4%)
    pallas_call x1, Pallas kernels, region_shards(): pl.pallas_call(region_kernel, out_shape=jax.ShapeDtypeStruct((part, local...  64 us
    unnamed x5, local copies, waits for them, and re-layouts  2.5 us

profile of v2, /device:TPU:0, one launch (start us, length us, event | category | flops | bytes accessed | tf_op | source)
XLA Modules:
  0.0 66.5 jit_solution(11147803158221065419)
XLA Ops:
  0.0 0.0 copy-start
  0.0 0.7 %copy-done = s32[48,12]{0,1:T(8,128)S(1)} copy-done((s32[48,12]{0,1:T(8,128)S(1)}, s32[48,12]{0,1:T(8,128)}, u32[]{:S(2)}) %copy-start) | copy-done | bytes 2328
  0.7 0.0 copy-start.1
  0.7 0.7 copy-done.1
  1.4 64.0 %shard_map.46 = f32[64,6144]{1,0:T(8,128)S(1)} custom-call(f32[64,6144]{1,0:T(8,128)} %own_ref.1, f32[64,6144]{1,0:T(8,128)} %weights_ref.1, s32[1,48]{1,0:T(1,128)S(1)} %bitcast.3, s32[12,48]{1,0:T(8,128)S(1)} %bitcast.2), custom_call_target="tpu_custom_call" | custom-call | tf_op jit(solution)/shard_map/pallas_call | solution.py:514
  65.4 1.1 %copy.6 = f32[64,6144]{1,0:T(8,128)} copy(f32[64,6144]{1,0:T(8,128)S(1)} %shard_map.46) | data formatting | bytes 3145728
Async XLA Ops:
  0.0 0.7 %copy-start = (s32[48,12]{0,1:T(8,128)S(1)}, s32[48,12]{0,1:T(8,128)}, u32[]{:S(2)}) copy-start(s32[48,12]{0,1:T(8,128)} %param.7) | copy-start | bytes 6916
  0.7 0.7 copy-start.1

commit v3 on v2

--- a/solution.py
+++ b/solution.py
@@ -470,9 +470,9 @@
 
         @pl.when(chunk == count - 4)
         def _():
+            forward(ends[1])
             work_close()
 
-    forward(ends[1])
     for side in range(2):
         relay(ends[0], side).wait_recv()
     prepare(count - 1, True, (0,))
@@ -511,6 +511,7 @@
     anywhere = pl.BlockSpec(memory_space=pltpu.HBM)
     dma = pltpu.SemaphoreType.DMA
     bf16, f32 = jnp.bfloat16, jnp.float32
+    operands = (states, weights, obs_count.reshape(1, tiles), neighbours.T)
     return pl.pallas_call(
         region_kernel,
         out_shape=jax.ShapeDtypeStruct((part, local_rows), f32),
@@ -543,7 +544,7 @@
         compiler_params=pltpu.CompilerParams(
             collective_id=0, has_side_effects=True, vmem_limit_bytes=52 * 1024 * 1024
         ),
-    )(states, weights, obs_count.reshape(1, tiles), neighbours.T)
+    )(*(pltpu.with_memory_space_constraint(value, pltpu.HBM) for value in operands))
 
 
 def fits(states, weights, obs_count, neighbours):

time: 66.7 us -> 64.2 us (0.963)
  local copies, waits for them, and re-layouts: 2.5 us -> 1.15 us
  Pallas kernels: 64 us -> 62.9 us
    unnamed x5 -> x1, local copies, waits for them, and re-layouts: 2.5 us -> 1.15 us
    pallas_call x1, Pallas kernels: 64 us -> 62.9 us  [region_shards(): pl.pallas_call(region_kernel, out_shape=jax.ShapeDtypeStruct((part, local...]
where the time goes in v3:
time: 64.2 us; the launch traced here: 64 us
  Pallas kernels  62.9 us (98%)
  local copies, waits for them, and re-layouts  1.15 us (2%)
    pallas_call x1, Pallas kernels, region_shards(): pl.pallas_call(region_kernel, out_shape=jax.ShapeDtypeStruct((part, local...  62.9 us

profile of v3, /device:TPU:0, one launch (start us, length us, event | category | flops | bytes accessed | tf_op | source)
XLA Modules:
  0.0 64.0 jit_solution(6174150676138461489)
XLA Ops:
  0.0 62.9 %shard_map.46 = f32[64,6144]{1,0:T(8,128)S(1)} custom-call(f32[64,6144]{1,0:T(8,128)} %own_ref.1, f32[64,6144]{1,0:T(8,128)} %weights_ref.1, s32[1,48]{1,0:T(1,128)} %bitcast.3, s32[12,48]{1,0:T(8,128)} %bitcast.2), custom_call_target="tpu_custom_call" | custom-call | tf_op jit(solution)/shard_map/pallas_call | solution.py:515
  62.9 1.1 %copy.6 = f32[64,6144]{1,0:T(8,128)} copy(f32[64,6144]{1,0:T(8,128)S(1)} %shard_map.46) | data formatting | bytes 3145728

commit v4 on v3

--- a/solution.py
+++ b/solution.py
@@ -245,7 +245,6 @@
     @pl.when(first)
     def _():
         signal(up_sem, above)
-        pl.semaphore_wait(down_sem, 1)
 
     @pl.when(last)
     def _():
@@ -256,12 +255,44 @@
     def _():
         pl.semaphore_wait(up_sem, 1)
         signal(up_sem, above)
+
+    @pl.when((region > 1) & jnp.logical_not(last))
+    def _():
         pl.semaphore_wait(down_sem, 1)
         signal(down_sem, below)
 
-    for item in (0, 1, 9, 8):
-        for up in (True, False):
-            rim(up, item).start()
+    at_once = (0, 1, 9, 8)
+    for item in at_once:
+        rim(True, item).start()
+
+    @pl.when(jnp.logical_not(first))
+    def _():
+        for item in at_once:
+            rim(False, item).start()
+
+    def late_start():
+        @pl.when(region == 1)
+        def _():
+            pl.semaphore_wait(down_sem, 1)
+            signal(down_sem, below)
+
+        @pl.when(first)
+        def _():
+            pl.semaphore_wait(down_sem, 1)
+            for item in at_once:
+                rim(False, item).start()
+            for slot in range(1, 4):
+                rim_of(0, slot).start()
+
+    def pass_on(step, slots):
+        def start():
+            for slot in slots:
+                rim_of(step, slot).start()
+
+        if step == 0:
+            pl.when(jnp.logical_not(first))(start)
+        else:
+            start()
 
     def prepare_weights(value, columns):
         high, low = split(value)
@@ -413,8 +444,7 @@
         for side in range(2):
             relay(step, side).start()
         if isinstance(step, int) and step < early:
-            for slot in (1, 2):
-                rim_of(step, slot).start()
+            pass_on(step, (1, 2))
 
     for chunk in range(count):
         own_copy(chunk).wait()
@@ -426,8 +456,10 @@
             direct(step + 3, side).start()
         for side in range(2):
             relay(step, side).wait_recv()
-        rim_of(step, 3).start()
+        pass_on(step, (3,))
         prepare(order[step] + 2, True)
+        if step == 0:
+            late_start()
         if step >= 2:
             work_edge(0 if step == 2 else pairs - 4)
 

time: 64.2 us -> 64.1 us (level)
  no operation moved by 1% of the time
where the time goes in v4:
time: 64.1 us; the launch traced here: 64 us
  Pallas kernels  62.9 us (98%)
  local copies, waits for them, and re-layouts  1.15 us (2%)
    pallas_call x1, Pallas kernels, region_shards(): pl.pallas_call(region_kernel, out_shape=jax.ShapeDtypeStruct((part, local...  62.9 us

profile of v4, /device:TPU:0, one launch (start us, length us, event | category | flops | bytes accessed | tf_op | source)
XLA Modules:
  0.0 64.0 jit_solution(10458888136073081301)
XLA Ops:
  0.0 62.9 %shard_map.46 = f32[64,6144]{1,0:T(8,128)S(1)} custom-call(f32[64,6144]{1,0:T(8,128)} %own_ref.1, f32[64,6144]{1,0:T(8,128)} %weights_ref.1, s32[1,48]{1,0:T(1,128)} %bitcast.3, s32[12,48]{1,0:T(8,128)} %bitcast.2), custom_call_target="tpu_custom_call" | custom-call | tf_op jit(solution)/shard_map/pallas_call | solution.py:547
  62.9 1.1 %copy.6 = f32[64,6144]{1,0:T(8,128)} copy(f32[64,6144]{1,0:T(8,128)S(1)} %shard_map.46) | data formatting | bytes 3145728
